TPU v7x, 32 devices: a whole 2x2x4 slice. The times are simulated.
32 devices in a mesh: replica: 16 (over z, y, core), fsdp: 2 (over x).
Axes of the slice: x: 2, y: 2, z: 4, core: 2. Of those that a mesh axis runs over, the one named last changes fastest.
Arguments:
- inner_weights: float32 [16, 3, 24, 6144], P('replica', None, None, 'fsdp'), may hold values from -8 to 8
- anchor: float32 [3, 24, 6144], P(None, None, 'fsdp'), may hold values from -4 to 4
- outer_moment: float32 [3, 24, 6144], P(None, None, 'fsdp'), may hold values from -3 to 3
- adam_first: float32 [16, 3, 24, 6144], P('replica', None, None, 'fsdp'), may hold values from -2 to 2
- adam_second: float32 [16, 3, 24, 6144], P('replica', None, None, 'fsdp'), may hold values from 0.1 to 1
- grad_parts: bfloat16 [16, 2, 3, 24, 6144], P('replica', 'fsdp'), may hold values from -2.5 to 2.5
Outputs:
- fresh_weights: bfloat16 [3, 24, 6144], replicated
- anchor_new: float32 [3, 24, 6144], P(None, None, 'fsdp')
- moment_new: float32 [3, 24, 6144], P(None, None, 'fsdp')
- first_new: float32 [16, 3, 24, 6144], P('replica', None, None, 'fsdp')
- second_new: float32 [16, 3, 24, 6144], P('replica', None, None, 'fsdp')
All inputs are finite; a program needn't handle non-finite values.
Results may differ from a plain program's by a relative error of at most 0.0025.
Values may be sent and summed in bfloat16 or wider, within the bound.
A program may use at most 64 MiB of HBM per device.

v0:
```python
import jax
import jax.numpy as jnp
from jax import lax
from jax.sharding import PartitionSpec as P

beta_one = 0.9
beta_two = 0.95
correct_one = 0.99997343860111
correct_two = 0.994079470779666
adam_eps = 1e-08
inner_rate = 0.1
decay_rate = 0.1
outer_rate = 0.7
outer_mu = 0.9


def inner_update(weights, anchor_now, first_now, second_now, gradient):
    first_new = beta_one * first_now + (1.0 - beta_one) * gradient
    second_new = beta_two * second_now + (1.0 - beta_two) * gradient * gradient
    update = first_new / correct_one / (jnp.sqrt(second_new / correct_two) + adam_eps)
    stepped = weights - inner_rate * (update + decay_rate * weights)
    return (first_new, second_new, anchor_now - stepped)


def outer_update(mean_delta, moment_now, anchor_now):
    moment_new = outer_mu * moment_now + mean_delta
    anchor_new = anchor_now - outer_rate * (mean_delta + outer_mu * moment_new)
    return (moment_new, anchor_new)


def per_device(inner_weights, anchor, outer_moment, adam_first, adam_second, grad_parts):
    received = lax.all_to_all(grad_parts, "fsdp", split_axis=4, concat_axis=1, tiled=True)
    gradient = jnp.sum(received.astype(jnp.float32), axis=1)
    first_new, second_new, pseudo = inner_update(
        inner_weights, anchor[None], adam_first, adam_second, gradient
    )
    pseudo = pseudo[0]
    workers = lax.axis_size("replica")
    summed = lax.psum(pseudo, "replica")
    moment_new, anchor_new = outer_update(summed / workers, outer_moment, anchor)
    fresh_weights = lax.all_gather(anchor_new.astype(jnp.bfloat16), "fsdp", axis=2, tiled=True)
    return (fresh_weights, anchor_new, moment_new, first_new, second_new)


def solution(mesh):
    in_specs = (
        P("replica", None, None, "fsdp"),
        P(None, None, "fsdp"),
        P(None, None, "fsdp"),
        P("replica", None, None, "fsdp"),
        P("replica", None, None, "fsdp"),
        P("replica", "fsdp", None, None, None),
    )
    out_specs = (
        P(),
        P(None, None, "fsdp"),
        P(None, None, "fsdp"),
        P("replica", None, None, "fsdp"),
        P("replica", None, None, "fsdp"),
    )
    return jax.shard_map(
        per_device, mesh=mesh, in_specs=in_specs, out_specs=out_specs, check_vma=False
    )
```

profile of v0, /device:TPU:0, one launch (start us, length us, event | category | flops | bytes accessed | tf_op | source)
XLA Modules:
  0.0 183.9 jit_solution(3862538814976636377)
XLA Ops:
  7.2 0.0 all-reduce.2.cloned.1.call-start
  7.2 8.0 %copy.50 = bf16[1,1,3,24,6144]{3,2,1,0,4:T(4,128)(2,1)} copy(bf16[1,1,3,24,6144]{4,3,2,1,0:T(8,128)(2,1)} %param.11) | data formatting | bytes 1769472 | tf_op args[5]
  15.3 8.1 %reshape.49 = bf16[2,2,110592]{2,1,0:T(2,128)(2,1)S(1)} reshape(bf16[6144,1,1,3,24]{4,3,2,1,0:T(4,128)(2,1)} %bitcast.18) | data formatting | bytes 1769472
  23.4 15.9 %all_to_all.4 = bf16[2,2,110592]{2,1,0:T(2,128)(2,1)S(1)} all-to-all(bf16[2,2,110592]{2,1,0:T(2,128)(2,1)S(1)} %reshape.49), channel_id=1, replica_groups=mesh['replica'=16,'fsdp'=2] {'fsdp'}, dimensions={0} | all-to-all | bytes 1769472 | tf_op jit(solution)/shard_map/all_to_all | solution.py:32
  39.3 8.9 %reshape.50 = bf16[6144,1,1,3,24]{4,3,2,1,0:T(4,128)(2,1)} reshape(bf16[2,2,110592]{2,1,0:T(2,128)(2,1)S(1)} %all_to_all.4) | data formatting | bytes 1769472
  48.1 11.1 %convert_reduce_fusion = f32[3,24,3072]{1,0,2:T(4,128)} fusion(bf16[3,24,2,3072]{1,0,3,2:T(4,128)(2,1)} %bitcast.17), kind=kLoop, calls=%fused_computation | loop fusion | flops 663552 | bytes 1769472 | tf_op jit(solution)/shard_map/reduce_sum | solution.py:33
  59.2 0.0 copy-start
  59.2 0.0 copy-start.1
  59.2 0.0 copy-start.2
  59.2 5.1 %copy.51 = f32[3,24,3072]{2,1,0:T(8,128)S(1)} copy(f32[3,24,3072]{1,0,2:T(4,128)} %convert_reduce_fusion) | data formatting | bytes 1769472 | tf_op jit(solution)/shard_map/reduce_sum | solution.py:33
  64.3 0.0 copy-done
  64.3 0.0 copy-done.1
  64.4 0.0 copy-done.2
  64.4 3.1 %fusion.2 = (f32[3,24,3072]{2,1,0:T(8,128)}, f32[1,3,24,3072]{3,2,1,0:T(8,128)}, f32[1,3,24,3072]{3,2,1,0:T(8,128)}) fusion(f32[3,24,3072]{2,1,0:T(8,128)S(1)} %copy-done, f32[1,3,24,3072]{3,2,1,0:T(8,128)S(1)} %copy-done.1, f32[3,24,3072]{2,1,0:T(8,128)S(1)} %copy.51, f32[1,3,24,3072]{3,2,1,0:T(8,128)S(1)} %copy-done.2, f32[1,3,24,3072]{3,2,1,0:T(8,128)} %param.10), kind=kLoop, calls=%fused_computation.6 | loop fusion | flops 3538944 | bytes 7077888 | tf_op jit(solution)/shard_map/squeeze | solution.py:37
  67.5 0.0 all-reduce.2.cloned.1.call-update
  67.5 94.0 %all-reduce.2.cloned.1.call-done = f32[3,24,3072]{2,1,0:T(8,128)} async-done(((f32[3,24,3072]{2,1,0:T(8,128)}), f32[3,24,3072]{2,1,0:T(8,128)}) %all-reduce.2.cloned.1.call-update) | async-done | bytes 884752 | tf_op jit(solution)/shard_map/psum | solution.py:39
  161.5 2.9 %fusion.3 = (bf16[3,24,3072]{2,1,0:T(8,128)(2,1)S(1)}, f32[3,24,3072]{2,1,0:T(8,128)}, f32[3,24,3072]{2,1,0:T(8,128)}) fusion(f32[3,24,3072]{2,1,0:T(8,128)S(1)} %copy-done, f32[3,24,3072]{2,1,0:T(8,128)} %all-reduce.2.cloned.1.call-done, f32[3,24,3072]{2,1,0:T(8,128)} %param.8), kind=kLoop, calls=%fused_computation.9 | loop fusion | flops 1769472 | bytes 4866048 | tf_op jit(solution)/shard_map/convert_element_type | solution.py:41
  164.4 11.7 %all_gather.3 = bf16[3,24,6144]{2,1,0:T(8,128)(2,1)S(1)} all-gather(bf16[3,24,3072]{2,1,0:T(8,128)(2,1)S(1)} %get-tuple-element.15), channel_id=1, replica_groups=mesh['replica'=16,'fsdp'=2] {'fsdp'}, dimensions={2}, use_global_device_ids=true | all-gather | bytes 1327104 | tf_op jit(solution)/shard_map/all_gather | solution.py:41
  176.1 0.9 copy.54
Async XLA Ops:
  7.2 154.3 %all-reduce.2.cloned.1.call-start = ((), (), s32[]{:S(2)}) async-start(), calls=%async_computation.1 | async-start | bytes 1769472 | tf_op jit(solution)/shard_map/psum | solution.py:39
  59.2 5.1 %copy-start = (f32[3,24,3072]{2,1,0:T(8,128)S(1)}, f32[3,24,3072]{2,1,0:T(8,128)}, u32[]{:S(2)}) copy-start(f32[3,24,3072]{2,1,0:T(8,128)} %param.7) | copy-start | bytes 2654212
  59.2 5.1 %copy-start.1 = (f32[1,3,24,3072]{3,2,1,0:T(8,128)S(1)}, f32[1,3,24,3072]{3,2,1,0:T(8,128)}, u32[]{:S(2)}) copy-start(f32[1,3,24,3072]{3,2,1,0:T(8,128)} %param.6) | copy-start | bytes 2654212
  59.2 5.1 %copy-start.2 = (f32[1,3,24,3072]{3,2,1,0:T(8,128)S(1)}, f32[1,3,24,3072]{3,2,1,0:T(8,128)}, u32[]{:S(2)}) copy-start(f32[1,3,24,3072]{3,2,1,0:T(8,128)} %param.9) | copy-start | bytes 2654212
Sparse Core Ops, SparseCore 0:
  67.6 93.8 all-reduce.1
where the time goes:
time: 185 us; the launch traced here: 184 us
  waiting for transfers between devices  94 us (51%)
  local copies, waits for them, and re-layouts  31.1 us (17%)
  blocking collectives  27.6 us (15%)
  other arithmetic  17.1 us (9%)
  between operations  14.1 us (8%)
    psum x1, waiting for transfers between devices, per_device(): summed = lax.psum(pseudo, 'replica')  94 us
    unnamed x10, local copies, waits for them, and re-layouts  26 us
    all_to_all x1, blocking collectives, per_device(): lax.all_to_all(grad_parts, 'fsdp', split_axis=4, concat_axis=1, tiled=True)  15.9 us
    all_gather x1, blocking collectives, per_device(): lax.all_gather(anchor_new.astype(jnp.bfloat16), 'fsdp', axis=2, tiled=True)  11.7 us
    reduce_sum x1, other arithmetic, per_device(): gradient = jnp.sum(received.astype(jnp.float32), axis=1)  11.1 us
    reduce_sum x1, local copies, waits for them, and re-layouts, per_device(): gradient = jnp.sum(received.astype(jnp.float32), axis=1)  5.09 us
  transfers between devices with their start and end apart: 1, of which 1 were waited for; matrix products, arithmetic and copies ran while one was open for 0% of the time, Pallas kernels for 0%

commit v1 on v0

--- a/solution.py
+++ b/solution.py
@@ -36,7 +36,8 @@
     )
     pseudo = pseudo[0]
     workers = lax.axis_size("replica")
-    summed = lax.psum(pseudo, "replica")
+    pieces = lax.all_gather(pseudo, "replica")
+    summed = jnp.sum(pieces, axis=0)
     moment_new, anchor_new = outer_update(summed / workers, outer_moment, anchor)
     fresh_weights = lax.all_gather(anchor_new.astype(jnp.bfloat16), "fsdp", axis=2, tiled=True)
     return (fresh_weights, anchor_new, moment_new, first_new, second_new)

time: 185 us -> 207 us (1.12)
  waiting for transfers between devices: 94 us -> 111 us
  other arithmetic: 17.1 us -> 21.7 us
    all_gather x0 -> x1, waiting for transfers between devices: none -> 111 us  [per_device(): pieces = lax.all_gather(pseudo, 'replica')]
    psum x1 -> x0, waiting for transfers between devices: 94 us -> none  [per_device(): summed = lax.psum(pseudo, 'replica')]
    reduce_sum x0 -> x1, other arithmetic: none -> 6.05 us  [per_device(): summed = jnp.sum(pieces, axis=0)]
    squeeze x1 -> x0, other arithmetic: 3.11 us -> none  [per_device(): pseudo = pseudo[0]]
    sub x0 -> x1, other arithmetic: none -> 3.11 us  [inner_update(): return (first_new, second_new, anchor_now - stepped)]
    unnamed x10 -> x12, local copies, waits for them, and re-layouts: 26 us -> 26 us
where the time goes in v1:
time: 207 us; the launch traced here: 206 us
  waiting for transfers between devices  111 us (54%)
  local copies, waits for them, and re-layouts  31.1 us (15%)
  blocking collectives  28.9 us (14%)
  other arithmetic  21.7 us (10%)
  between operations  14.1 us (7%)
    all_gather x1, waiting for transfers between devices, per_device(): pieces = lax.all_gather(pseudo, 'replica')  111 us
    unnamed x12, local copies, waits for them, and re-layouts  26 us
    all_to_all x1, blocking collectives, per_device(): lax.all_to_all(grad_parts, 'fsdp', split_axis=4, concat_axis=1, tiled=True)  16 us
    all_gather x1, blocking collectives, per_device(): lax.all_gather(anchor_new.astype(jnp.bfloat16), 'fsdp', axis=2, tiled=True)  13 us
    reduce_sum x1, other arithmetic, per_device(): gradient = jnp.sum(received.astype(jnp.float32), axis=1)  11.1 us
    reduce_sum x1, other arithmetic, per_device(): summed = jnp.sum(pieces, axis=0)  6.05 us
    reduce_sum x1, local copies, waits for them, and re-layouts, per_device(): gradient = jnp.sum(received.astype(jnp.float32), axis=1)  5.09 us
  transfers between devices with their start and end apart: 1, of which 1 were waited for; matrix products, arithmetic and copies ran while one was open for 0% of the time, Pallas kernels for 0%

profile of v1, /device:TPU:0, one launch (start us, length us, event | category | flops | bytes accessed | tf_op | source)
XLA Modules:
  0.0 206.5 jit_solution(5544960593438542141)
XLA Ops:
  7.2 0.0 all-gather.2.cloned.1.call-start
  7.2 8.1 %copy.26 = bf16[1,1,3,24,6144]{3,2,1,0,4:T(4,128)(2,1)} copy(bf16[1,1,3,24,6144]{4,3,2,1,0:T(8,128)(2,1)} %param.11) | data formatting | bytes 1769472 | tf_op args[5]
  15.3 8.1 %reshape.49 = bf16[2,2,110592]{2,1,0:T(2,128)(2,1)S(1)} reshape(bf16[6144,1,1,3,24]{4,3,2,1,0:T(4,128)(2,1)} %bitcast.14) | data formatting | bytes 1769472
  23.4 16.0 %all_to_all.4 = bf16[2,2,110592]{2,1,0:T(2,128)(2,1)S(1)} all-to-all(bf16[2,2,110592]{2,1,0:T(2,128)(2,1)S(1)} %reshape.49), channel_id=1, replica_groups=mesh['replica'=16,'fsdp'=2] {'fsdp'}, dimensions={0} | all-to-all | bytes 1769472 | tf_op jit(solution)/shard_map/all_to_all | solution.py:32
  39.4 8.8 %reshape.50 = bf16[6144,1,1,3,24]{4,3,2,1,0:T(4,128)(2,1)} reshape(bf16[2,2,110592]{2,1,0:T(2,128)(2,1)S(1)} %all_to_all.4) | data formatting | bytes 1769472
  48.2 11.1 %convert_reduce_fusion = f32[3,24,3072]{1,0,2:T(4,128)} fusion(bf16[3,24,2,3072]{1,0,3,2:T(4,128)(2,1)} %bitcast.13), kind=kLoop, calls=%fused_computation | loop fusion | flops 663552 | bytes 1769472 | tf_op jit(solution)/shard_map/reduce_sum | solution.py:33
  59.3 0.0 copy-start
  59.3 0.0 copy-start.1
  59.3 0.0 copy-start.2
  59.3 5.1 %copy.27 = f32[3,24,3072]{2,1,0:T(8,128)S(1)} copy(f32[3,24,3072]{1,0,2:T(4,128)} %convert_reduce_fusion) | data formatting | bytes 1769472 | tf_op jit(solution)/shard_map/reduce_sum | solution.py:33
  64.4 0.0 copy-done
  64.4 0.0 copy-done.1
  64.4 0.0 copy-done.2
  64.4 3.1 %bitcast_subtract_fusion = (f32[1,3,24,3072]{3,2,1,0:T(8,128)}, f32[1,3,24,3072]{3,2,1,0:T(8,128)}, f32[1,3,24,3072]{3,2,1,0:T(8,128)}) fusion(f32[3,24,3072]{2,1,0:T(8,128)S(1)} %copy-done, f32[1,3,24,3072]{3,2,1,0:T(8,128)S(1)} %copy-done.1, f32[3,24,3072]{2,1,0:T(8,128)S(1)} %copy.27, f32[1,3,24,3072]{3,2,1,0:T(8,128)S(1)} %copy-done.2, ...), kind=kLoop, calls=%fused_computation.5 | loop fusion | flops 3538944 | bytes 7077888 | tf_op jit(solution)/shard_map/sub | solution.py:22
  67.5 0.0 all-gather.2.cloned.1.call-update
  67.6 0.0 copy-start.3
  67.6 110.6 %all-gather.2.cloned.1.call-done = f32[16,3,24,3072]{3,2,1,0:T(8,128)} async-done(((f32[1,3,24,3072]{3,2,1,0:T(8,128)}), f32[16,3,24,3072]{3,2,1,0:T(8,128)}) %all-gather.2.cloned.1.call-update) | async-done | bytes 14155792 | tf_op jit(solution)/shard_map/all_gather | solution.py:39
  178.2 6.0 %reduce_sum.22 = f32[3,24,3072]{2,1,0:T(8,128)S(1)} reduce(f32[16,3,24,3072]{3,2,1,0:T(8,128)} %all-gather.2.cloned.1.call-done, f32[]{:T(128)} %constant.3.clone.1), dimensions={0}, to_apply=%region_1.0 | reduce | flops 3317760 | bytes 15040516 | tf_op jit(solution)/shard_map/reduce_sum | solution.py:40
  184.3 0.0 copy-done.3
  184.3 1.5 fusion.2
  185.7 13.0 %all_gather.7 = bf16[3,24,6144]{2,1,0:T(8,128)(2,1)S(1)} all-gather(bf16[3,24,3072]{2,1,0:T(8,128)(2,1)S(1)} %get-tuple-element.10), channel_id=1, replica_groups=mesh['replica'=16,'fsdp'=2] {'fsdp'}, dimensions={2}, use_global_device_ids=true | all-gather | bytes 1327104 | tf_op jit(solution)/shard_map/all_gather | solution.py:42
  198.7 0.9 copy.29
Async XLA Ops:
  7.2 171.1 %all-gather.2.cloned.1.call-start = ((), (), s32[]{:S(2)}) async-start(), calls=%async_computation.1 | async-start | bytes 15040512 | tf_op jit(solution)/shard_map/all_gather | solution.py:39
  59.3 5.1 %copy-start = (f32[3,24,3072]{2,1,0:T(8,128)S(1)}, f32[3,24,3072]{2,1,0:T(8,128)}, u32[]{:S(2)}) copy-start(f32[3,24,3072]{2,1,0:T(8,128)} %param.7) | copy-start | bytes 2654212
  59.3 5.1 %copy-start.1 = (f32[1,3,24,3072]{3,2,1,0:T(8,128)S(1)}, f32[1,3,24,3072]{3,2,1,0:T(8,128)}, u32[]{:S(2)}) copy-start(f32[1,3,24,3072]{3,2,1,0:T(8,128)} %param.6) | copy-start | bytes 2654212
  59.3 5.1 %copy-start.2 = (f32[1,3,24,3072]{3,2,1,0:T(8,128)S(1)}, f32[1,3,24,3072]{3,2,1,0:T(8,128)}, u32[]{:S(2)}) copy-start(f32[1,3,24,3072]{3,2,1,0:T(8,128)} %param.9) | copy-start | bytes 2654212
  67.6 116.7 %copy-start.3 = (f32[3,24,3072]{2,1,0:T(8,128)S(1)}, f32[3,24,3072]{2,1,0:T(8,128)}, u32[]{:S(2)}) copy-start(f32[3,24,3072]{2,1,0:T(8,128)} %param.8) | copy-start | bytes 2654212
Sparse Core Ops, SparseCore 0:
  67.7 110.4 all-gather.1
